TPU v7x, 32 devices: a whole 2x2x4 slice. The times are simulated.
32 devices in a mesh: expert: 8 (over z, y), tensor: 4 (over x, core).
Axes of the slice: x: 2, y: 2, z: 4, core: 2. Of those that a mesh axis runs over, the one named last changes fastest.
Arguments:
- tokens: bfloat16 [1024, 7168], P('expert', 'tensor'), may hold values from -6 to 6
- out_grad: bfloat16 [1024, 7168], P('expert', 'tensor'), may hold values from -1.5 to 1.5
- expert_ids: int32 [1024, 2], P('expert'), may hold values from 0 to 7, all different within a row; in each aligned block of 128 rows (0 to 127, 128 to 255, ...) at most 48 rows name the same one
- gate_values: bfloat16 [1024, 2], P('expert'), may hold values from 0.099609375 to 1
- w_gate: bfloat16 [8, 7168, 1024], P('expert', None, 'tensor'), may hold values from -0.0625 to 0.0625
- w_up: bfloat16 [8, 7168, 1024], P('expert', None, 'tensor'), may hold values from -0.0625 to 0.0625
- w_down: bfloat16 [8, 1024, 7168], P('expert', 'tensor'), may hold values from -0.1875 to 0.1875
Outputs:
- d_tokens: bfloat16 [1024, 7168], P('expert', 'tensor')
- d_gates: float32 [1024, 2], P('expert')
Inputs may be any that keep to these rules, and one draw needn't show every extreme that they name: `expert_ids`: each row names 2 different experts. Among the 128 rows held at one index along `expert` (one aligned block) no expert is named by more than 48 rows, and in some such block one expert is named by exactly 48.
All inputs are finite; a program needn't handle non-finite values.
Results may differ from a plain program's by a relative error of at most 0.0049.
Values may be sent and summed in bfloat16 or wider, within the bound.
A program may use at most 128 MiB of HBM per device.

v0:
```python
import jax
import jax.numpy as jnp
from jax import lax
from jax.sharding import PartitionSpec as P


def local(tokens, out_grad, expert_ids, gate_values, w_gate, w_up, w_down):
    n_experts = lax.axis_size("expert")
    tok_rows, quarter = tokens.shape
    top_count = expert_ids.shape[1]
    most_slots = 3 * tok_rows * top_count // (2 * n_experts)
    slot_count = n_experts * most_slots
    flat_ids = expert_ids.reshape(-1)
    onehot = (flat_ids[:, None] == jnp.arange(n_experts, dtype=jnp.int32)[None, :]).astype(
        jnp.int32
    )
    before = jnp.cumsum(onehot, axis=0) - onehot
    rank = jnp.sum(before * onehot, axis=1)
    slot_of = (flat_ids * most_slots + rank).reshape(tok_rows, top_count)
    matches = slot_of[None, :, :] == jnp.arange(slot_count, dtype=jnp.int32)[:, None, None]
    chooser = jnp.any(matches, axis=2).astype(jnp.bfloat16)
    send_x = jnp.dot(chooser, tokens, preferred_element_type=jnp.float32).astype(jnp.bfloat16)
    send_dy = jnp.dot(chooser, out_grad, preferred_element_type=jnp.float32).astype(jnp.bfloat16)
    gate_wide = gate_values.astype(jnp.float32)[None, :, :]
    send_g = jnp.sum(jnp.where(matches, gate_wide, 0.0), axis=(1, 2)).astype(jnp.bfloat16)
    recv_x, recv_dy, recv_g = (
        lax.all_to_all(
            send_x.reshape(n_experts, most_slots, quarter),
            "expert",
            split_axis=0,
            concat_axis=0,
            tiled=True,
        ),
        lax.all_to_all(
            send_dy.reshape(n_experts, most_slots, quarter),
            "expert",
            split_axis=0,
            concat_axis=0,
            tiled=True,
        ),
        lax.all_to_all(
            send_g.reshape(n_experts, most_slots), "expert", split_axis=0, concat_axis=0, tiled=True
        ),
    )
    rows_x = recv_x.reshape(slot_count, quarter)
    rows_dy = recv_dy.reshape(slot_count, quarter)
    gate_mat = w_gate[0]
    up_mat = w_up[0]
    down_mat = w_down[0]
    piece_x = lax.all_gather(rows_x, "tensor", axis=1, tiled=True)
    piece_dy = lax.all_gather(rows_dy, "tensor", axis=1, tiled=True)
    pre_sum = jnp.dot(piece_x, gate_mat, preferred_element_type=jnp.float32)
    up_sum = jnp.dot(piece_x, up_mat, preferred_element_type=jnp.float32)
    grad_sum = lax.dot_general(
        piece_dy, down_mat, (((1,), (1,)), ((), ())), preferred_element_type=jnp.float32
    )
    sigma = jax.nn.sigmoid(pre_sum)
    active = pre_sum * sigma
    partial_grad = jnp.sum(active * up_sum * grad_sum, axis=1)
    weight_g = recv_g.reshape(slot_count).astype(jnp.float32)
    scaled = weight_g[:, None] * grad_sum
    grad_up = (scaled * active).astype(jnp.bfloat16)
    grad_pre = (scaled * up_sum * sigma * (1.0 + pre_sum * (1.0 - sigma))).astype(jnp.bfloat16)
    contrib = lax.dot_general(
        grad_pre, gate_mat, (((1,), (1,)), ((), ())), preferred_element_type=jnp.float32
    )
    contrib = contrib + lax.dot_general(
        grad_up, up_mat, (((1,), (1,)), ((), ())), preferred_element_type=jnp.float32
    )
    slot_grad = lax.psum(partial_grad, "tensor")
    returned, returned_grad = (
        lax.all_to_all(
            contrib.reshape(n_experts, most_slots, contrib.shape[1]),
            "expert",
            split_axis=0,
            concat_axis=0,
            tiled=True,
        ),
        lax.all_to_all(
            slot_grad.reshape(n_experts, most_slots),
            "expert",
            split_axis=0,
            concat_axis=0,
            tiled=True,
        ),
    )
    slot_rows = returned.reshape(slot_count, contrib.shape[1])
    combined = jnp.sum(jnp.take(slot_rows, slot_of, axis=0), axis=1)
    d_tokens = lax.psum_scatter(combined, "tensor", scatter_dimension=1, tiled=True).astype(
        jnp.bfloat16
    )
    d_gates = jnp.take(returned_grad.reshape(slot_count), slot_of, axis=0)
    return (d_tokens, d_gates)


def solution(mesh):
    placed = (
        P("expert", "tensor"),
        P("expert", "tensor"),
        P("expert", None),
        P("expert", None),
        P("expert", None, "tensor"),
        P("expert", None, "tensor"),
        P("expert", "tensor", None),
    )
    return jax.shard_map(
        local,
        mesh=mesh,
        in_specs=placed,
        out_specs=(P("expert", "tensor"), P("expert", None)),
        check_vma=False,
    )
```

profile of v0, /device:TPU:0, one launch (start us, length us, event | category | flops | bytes accessed | tf_op | source)
XLA Modules:
  0.0 491.3 jit_solution(14696424435222848767)
XLA Ops:
  7.2 0.9 copy.32
  8.2 0.1 eq.38
  8.4 0.6 reduce-window.6
  9.0 0.2 slice_reduce_fusion
  9.3 0.1 reduce_sum.39
  9.5 0.7 compare_select_fusion
  10.3 0.5 convolution_convert_fusion
  10.8 40.6 %all_to_all.30 = bf16[8,48,1792]{2,1,0:T(8,128)(2,1)} all-to-all(bf16[8,48,1792]{2,1,0:T(8,128)(2,1)S(1)} %bitcast.40), channel_id=1, replica_groups=mesh['expert'=8,'tensor'=4] {'expert'}, dimensions={0} | all-to-all | bytes 2752512 | tf_op jit(solution)/shard_map/all_to_all | solution.py:27
  51.5 0.5 convolution_convert_fusion.1
  52.0 36.1 %all_to_all.31 = bf16[8,48,1792]{2,1,0:T(8,128)(2,1)} all-to-all(bf16[8,48,1792]{2,1,0:T(8,128)(2,1)S(1)} %bitcast.39), channel_id=1, replica_groups=mesh['expert'=8,'tensor'=4] {'expert'}, dimensions={0} | all-to-all | bytes 2752512 | tf_op jit(solution)/shard_map/all_to_all | solution.py:34
  88.2 0.1 select_reduce_fusion.1
  88.4 9.2 %all_to_all.32 = bf16[8,1,48]{2,1,0:T(2,128)(2,1)S(1)} all-to-all(bf16[8,1,48]{2,1,0:T(2,128)(2,1)S(1)} %convert_element_type.63), channel_id=1, replica_groups=mesh['expert'=8,'tensor'=4] {'expert'}, dimensions={0} | all-to-all | bytes 1536 | tf_op jit(solution)/shard_map/all_to_all | solution.py:41
  97.7 6.8 %fusion.2 = f32[384,256]{0,1:T(8,128)S(1)} fusion(bf16[384,7168]{1,0:T(8,128)(2,1)} %all-gather.5.cloned.1.call-done, bf16[1,7168,256]{2,1,0:T(8,128)(2,1)} %param.11), kind=kOutput, calls=%fused_computation.6 | convolution fusion | flops 1409286144 | bytes 9568256 | tf_op jit(solution)/shard_map/dot_general | solution.py:52
  104.5 1.4 copy-done.5
  105.9 2.1 fusion.5
  108.0 27.4 %all-gather.3.cloned.1.call-done = bf16[384,7168]{1,0:T(8,128)(2,1)} async-done(((bf16[384,1792]{1,0:T(8,128)(2,1)}), bf16[384,7168]{1,0:T(8,128)(2,1)}) %all-gather.3.cloned.1.call-update) | async-done | bytes 5505040 | tf_op jit(solution)/shard_map/all_gather | solution.py:51
  135.4 5.8 %multiply_reduce_fusion = (f32[384]{0:T(512)S(1)}, f32[384,256]{0,1:T(8,128)S(1)}) fusion(f32[384,256]{0,1:T(8,128)S(1)} %fusion.5, f32[384,256]{0,1:T(8,128)S(1)} %fusion.2, bf16[384,7168]{1,0:T(8,128)(2,1)} %all-gather.3.cloned.1.call-done, bf16[1,256,7168]{2,1,0:T(8,128)(2,1)} %param.13), kind=kOutput, calls=%fused_computation.15 | convolution fusion | flops 1409973888 | bytes 10356224 | tf_op jit(solution)/shard_map/dot_general | solution.py:54
  141.3 6.5 %psum.7 = f32[8,1,48]{2,1,0:T(1,128)} all-reduce(f32[8,1,48]{2,1,0:T(1,128)S(1)} %all_to_all.23), channel_id=1, replica_groups=mesh['expert'=8,'tensor'=4] {'tensor'}, use_global_device_ids=true, to_apply=%region_8.9 | all-reduce | flops 384 | bytes 3072 | tf_op jit(solution)/shard_map/psum | solution.py:70
  147.8 5.7 %all-to-all-start.4 = ((f32[8,1,48]{2,1,0:T(1,128)}), f32[8,1,48]{2,1,0:T(1,128)S(1)}, u32[]{:S(2)}, u32[]{:S(2)}) async-start(f32[8,1,48]{2,1,0:T(1,128)} %psum.7), calls=%async_computation.5 | async-start | bytes 8192 | tf_op jit(solution)/shard_map/all_to_all | solution.py:79
  153.4 4.0 fusion
  157.4 5.7 %convolution_add_fusion = f32[384,7168]{1,0:T(8,128)} fusion(f32[384,7168]{1,0:T(8,128)S(1)} %fusion, bf16[1,7168,256]{2,1,0:T(8,128)(2,1)S(1)} %copy-done.3, f32[384,256]{0,1:T(8,128)S(1)} %get-tuple-element.13, f32[384]{0:T(512)S(1)} %reshape.94, f32[384,256]{0,1:T(8,128)S(1)} %fusion.2), kind=kOutput, calls=%fused_computation.2 | convolution fusion | flops 1412726784 | bytes 26478080 | tf_op jit(solution)/shard_map/dot_general | solution.py:67
  163.1 6.0 %all-to-all-start.3 = ((f32[8,48,7168]{2,1,0:T(8,128)}), f32[8,48,7168]{2,1,0:T(8,128)}, u32[]{:S(2)}, u32[]{:S(2)}) async-start(f32[8,48,7168]{2,1,0:T(8,128)} %bitcast.36), calls=%async_computation.3 | async-start | bytes 22020096 | tf_op jit(solution)/shard_map/all_to_all | solution.py:72
  169.4 0.5 broadcast.53
  170.0 0.7 reduce.9
  170.7 1.9 gather_fusion.1
  172.9 0.6 broadcast_select_fusion
  173.6 233.9 %all-to-all-done.3 = f32[8,48,7168]{2,1,0:T(8,128)} async-done(((f32[8,48,7168]{2,1,0:T(8,128)}), f32[8,48,7168]{2,1,0:T(8,128)}, u32[]{:S(2)}, u32[]{:S(2)}) %all-to-all-start.3) | async-done | bytes 11010080 | tf_op jit(solution)/shard_map/all_to_all | solution.py:72
  407.5 13.0 %gather_fusion = f32[256,7168]{1,0:T(8,128)} fusion(f32[384,7168]{1,0:T(8,128)} %bitcast.10, s32[1024]{0:T(1024)S(1)} %pad_clamp_fusion), kind=kCustom, calls=%fused_computation | custom fusion | bytes 14681088 | tf_op jit(solution)/shard_map/jit(_take)/gather | solution.py:88
  420.5 9.3 %reshape.96 = f32[128,2,7168]{2,1,0:T(2,128)} reshape(f32[256,7168]{1,0:T(8,128)} %gather_fusion) | data formatting | bytes 14680064 | tf_op jit(solution)/shard_map/jit(_take)/gather | solution.py:88
  429.8 13.4 %select_reduce_fusion = f32[128,7168]{1,0:T(8,128)} fusion(f32[128,2,7168]{2,1,0:T(2,128)} %reshape.96, pred[128,2]{1,0:T(8,128)(4,1)S(1)} %copy.35), kind=kLoop, calls=%fused_computation.3 | loop fusion | flops 2752512 | bytes 11010304 | tf_op jit(solution)/shard_map/reduce_sum | solution.py:88
  443.2 39.5 %reduce-scatter.2.cloned.1.call-done = f32[128,1792]{1,0:T(8,128)} async-done(((f32[128,7168]{1,0:T(8,128)}), f32[128,1792]{1,0:T(8,128)}) %reduce-scatter.2.cloned.1.call-update) | async-done | bytes 917520 | tf_op jit(solution)/shard_map/reduce_scatter | solution.py:89
  482.8 2.0 convert_element_type.61
  (40 shorter events, 1.5 us)
Async XLA Ops:
  7.2 3.1 copy-start
  7.2 44.3 %copy-start.4 = (bf16[128,1792]{1,0:T(8,128)(2,1)S(1)}, bf16[128,1792]{1,0:T(8,128)(2,1)}, u32[]{:S(2)}) copy-start(bf16[128,1792]{1,0:T(8,128)(2,1)} %param.8) | copy-start | bytes 1376260
  7.2 90.5 %all-gather.5.cloned.1.call-start = ((), (), s32[]{:S(2)}) async-start(), calls=%async_computation.7 | async-start | bytes 6881280 | tf_op jit(solution)/shard_map/all_gather | solution.py:50
  51.4 36.7 %copy-start.6 = (bf16[128,2]{0,1:T(2,128)(2,1)S(1)}, bf16[128,2]{0,1:T(2,128)(2,1)}, u32[]{:S(2)}) copy-start(bf16[128,2]{0,1:T(2,128)(2,1)} %param.10) | copy-start | bytes 1540
  51.4 84.0 %all-gather.3.cloned.1.call-start = ((), (), s32[]{:S(2)}) async-start(), calls=%async_computation.6 | async-start | bytes 6881280 | tf_op jit(solution)/shard_map/all_gather | solution.py:51
  97.7 6.8 %copy-start.2 = (bf16[1,7168,256]{2,1,0:T(8,128)(2,1)S(1)}, bf16[1,7168,256]{2,1,0:T(8,128)(2,1)}, u32[]{:S(2)}) copy-start(bf16[1,7168,256]{2,1,0:T(8,128)(2,1)} %param.12) | copy-start | bytes 11010052
  97.7 8.2 %copy-start.5 = (bf16[384,7168]{1,0:T(8,128)(2,1)S(1)}, bf16[384,7168]{1,0:T(8,128)(2,1)}, u32[]{:S(2)}) copy-start(bf16[384,7168]{1,0:T(8,128)(2,1)} %all-gather.5.cloned.1.call-done) | copy-start | bytes 16515076
  147.8 15.4 %all-to-all-start.4 = ((f32[8,1,48]{2,1,0:T(1,128)}), f32[8,1,48]{2,1,0:T(1,128)S(1)}, u32[]{:S(2)}, u32[]{:S(2)}) async-start(f32[8,1,48]{2,1,0:T(1,128)} %psum.7), calls=%async_computation.5 | async-start | bytes 8192 | tf_op jit(solution)/shard_map/all_to_all | solution.py:79
  153.4 4.0 copy-start.3
  163.1 244.4 %all-to-all-start.3 = ((f32[8,48,7168]{2,1,0:T(8,128)}), f32[8,48,7168]{2,1,0:T(8,128)}, u32[]{:S(2)}, u32[]{:S(2)}) async-start(f32[8,48,7168]{2,1,0:T(8,128)} %bitcast.36), calls=%async_computation.3 | async-start | bytes 22020096 | tf_op jit(solution)/shard_map/all_to_all | solution.py:72
  169.1 313.7 %reduce-scatter.2.cloned.1.call-start = ((), (), s32[]{:S(2)}) async-start(), calls=%async_computation.8 | async-start | bytes 4587520 | tf_op jit(solution)/shard_map/reduce_scatter | solution.py:89
  429.8 55.0 %copy-start.1 = (bf16[128,1792]{1,0:T(8,128)(2,1)S(1)}, bf16[128,1792]{1,0:T(8,128)(2,1)}, u32[]{:S(2)}) copy-start(bf16[128,1792]{1,0:T(8,128)(2,1)} %param.7) | copy-start | bytes 1376260
Sparse Core Ops, SparseCore 0:
  51.6 40.2 all-gather.4
  93.5 41.9 all-gather.2
  443.4 39.3 reduce-scatter.1
where the time goes:
time: 492 us; the launch traced here: 491 us
  waiting for transfers between devices  301 us (61%)
  blocking collectives  92.4 us (19%)
  local copies, waits for them, and re-layouts  28.6 us (6%)
  matrix products  25.3 us (5%)
  other arithmetic  18.3 us (4%)
  between operations  13.9 us (3%)
  starting transfers between devices  11.8 us (2%)
    all_to_all x1, waiting for transfers between devices, local(): lax.all_to_all(contrib.reshape(n_experts, most_slots, contrib.shape[1]),...  234 us
    all_to_all x1, blocking collectives, local(): lax.all_to_all(send_x.reshape(n_experts, most_slots, quarter), 'expert',...  40.6 us
    reduce_scatter x1, waiting for transfers between devices, local(): lax.psum_scatter(combined, 'tensor', scatter_dimension=1, tiled=True)  39.5 us
    all_to_all x1, blocking collectives, local(): lax.all_to_all(send_dy.reshape(n_experts, most_slots, quarter), 'expert',...  36.1 us
    all_gather x1, waiting for transfers between devices, local(): piece_dy = lax.all_gather(rows_dy, 'tensor', axis=1, tiled=True)  27.4 us
    gather x2, local copies, waits for them, and re-layouts, local(): combined = jnp.sum(jnp.take(slot_rows, slot_of, axis=0), axis=1)  22.2 us
    reduce_sum x1, other arithmetic, local(): combined = jnp.sum(jnp.take(slot_rows, slot_of, axis=0), axis=1)  13.4 us
  transfers between devices with their start and end apart: 5, of which 3 were waited for; matrix products, arithmetic and copies ran while one was open for 5% of the time, Pallas kernels for 0%

commit v1 on v0

--- a/solution.py
+++ b/solution.py
@@ -47,8 +47,11 @@
     gate_mat = w_gate[0]
     up_mat = w_up[0]
     down_mat = w_down[0]
-    piece_x = lax.all_gather(rows_x, "tensor", axis=1, tiled=True)
-    piece_dy = lax.all_gather(rows_dy, "tensor", axis=1, tiled=True)
+    piece_x, piece_dy = jnp.split(
+        lax.all_gather(jnp.concatenate([rows_x, rows_dy], axis=0), "tensor", axis=1, tiled=True),
+        [rows_x.shape[0]],
+        axis=0,
+    )
     pre_sum = jnp.dot(piece_x, gate_mat, preferred_element_type=jnp.float32)
     up_sum = jnp.dot(piece_x, up_mat, preferred_element_type=jnp.float32)
     grad_sum = lax.dot_general(

time: 492 us -> 527 us (1.071)
  waiting for transfers between devices: 301 us -> 367 us
  blocking collectives: 92.4 us -> 52.7 us
  starting transfers between devices: 11.8 us -> 19 us
    all_to_all x1 -> x0, blocking collectives: 40.6 us -> none  [local(): lax.all_to_all(send_x.reshape(n_experts, most_slots, quarter), 'expert',...]
    all_gather x2 -> x1, waiting for transfers between devices: 27.4 us -> 62.1 us  [local(): lax.all_gather(jnp.concatenate([rows_x, rows_dy], axis=0), 'tensor', axis...]
    all_to_all x0 -> x1, waiting for transfers between devices: none -> 31.2 us  [local(): lax.all_to_all(send_x.reshape(n_experts, most_slots, quarter), 'expert',...]
    all_to_all x0 -> x1, starting transfers between devices: none -> 7.28 us  [local(): lax.all_to_all(send_x.reshape(n_experts, most_slots, quarter), 'expert',...]
  transfers between devices with their start and end apart: 5 -> 5, of which waited for: 3 -> 4; matrix products, arithmetic and copies ran while one was open for 5% -> 3% of each run, Pallas kernels for 0% -> 0%
where the time goes in v1:
time: 527 us; the launch traced here: 526 us
  waiting for transfers between devices  367 us (70%)
  blocking collectives  52.7 us (10%)
  local copies, waits for them, and re-layouts  27.2 us (5%)
  matrix products  25.7 us (5%)
  other arithmetic  20.1 us (4%)
  starting transfers between devices  19 us (4%)
  between operations  14.3 us (3%)
    all_to_all x1, waiting for transfers between devices, local(): lax.all_to_all(contrib.reshape(n_experts, most_slots, contrib.shape[1]),...  234 us
    all_gather x1, waiting for transfers between devices, local(): lax.all_gather(jnp.concatenate([rows_x, rows_dy], axis=0), 'tensor', axis...  62.1 us
    reduce_scatter x1, waiting for transfers between devices, local(): lax.psum_scatter(combined, 'tensor', scatter_dimension=1, tiled=True)  39.5 us
    all_to_all x1, blocking collectives, local(): lax.all_to_all(send_dy.reshape(n_experts, most_slots, quarter), 'expert',...  37 us
    all_to_all x1, waiting for transfers between devices, local(): lax.all_to_all(send_x.reshape(n_experts, most_slots, quarter), 'expert',...  31.2 us
    gather x2, local copies, waits for them, and re-layouts, local(): combined = jnp.sum(jnp.take(slot_rows, slot_of, axis=0), axis=1)  22.2 us
    reduce_sum x1, other arithmetic, local(): combined = jnp.sum(jnp.take(slot_rows, slot_of, axis=0), axis=1)  13.4 us
  transfers between devices with their start and end apart: 5, of which 4 were waited for; matrix products, arithmetic and copies ran while one was open for 3% of the time, Pallas kernels for 0%

profile of v1, /device:TPU:0, one launch (start us, length us, event | category | flops | bytes accessed | tf_op | source)
XLA Modules:
  0.0 525.9 jit_solution(10138759243282469262)
XLA Ops:
  7.2 0.8 copy.32
  8.3 0.6 reduce-window.6
  8.9 0.2 slice_reduce_fusion
  9.3 0.1 reduce_sum.39
  9.5 0.7 compare_select_fusion
  10.2 1.6 convolution_convert_fusion.1
  11.8 7.3 %all-to-all-start.1 = ((bf16[8,48,1792]{2,1,0:T(8,128)(2,1)}), bf16[8,48,1792]{2,1,0:T(8,128)(2,1)S(1)}, u32[]{:S(2)}, u32[]{:S(2)}) async-start(bf16[8,48,1792]{2,1,0:T(8,128)(2,1)} %bitcast.2), calls=%async_computation.1 | async-start | bytes 2752512 | tf_op jit(solution)/shard_map/all_to_all | solution.py:27
  19.1 1.5 convolution_convert_fusion
  20.7 31.2 %all-to-all-done.1 = bf16[8,48,1792]{2,1,0:T(8,128)(2,1)S(1)} async-done(((bf16[8,48,1792]{2,1,0:T(8,128)(2,1)}), bf16[8,48,1792]{2,1,0:T(8,128)(2,1)S(1)}, u32[]{:S(2)}, u32[]{:S(2)}) %all-to-all-start.1) | async-done | bytes 1376288 | tf_op jit(solution)/shard_map/all_to_all | solution.py:27
  51.9 37.0 %all_to_all.30 = bf16[8,48,1792]{2,1,0:T(8,128)(2,1)S(1)} all-to-all(bf16[8,48,1792]{2,1,0:T(8,128)(2,1)S(1)} %bitcast.35), channel_id=1, replica_groups=mesh['expert'=8,'tensor'=4] {'expert'}, dimensions={0} | all-to-all | bytes 2752512 | tf_op jit(solution)/shard_map/all_to_all | solution.py:34
  88.9 1.8 pad_maximum_fusion
  90.7 0.1 select_reduce_fusion.1
  91.0 9.3 %all_to_all.31 = bf16[8,1,48]{2,1,0:T(2,128)(2,1)S(1)} all-to-all(bf16[8,1,48]{2,1,0:T(2,128)(2,1)S(1)} %convert_element_type.63), channel_id=1, replica_groups=mesh['expert'=8,'tensor'=4] {'expert'}, dimensions={0} | all-to-all | bytes 1536 | tf_op jit(solution)/shard_map/all_to_all | solution.py:41
  100.3 62.1 %all-gather.2.cloned.1.call-done = bf16[768,7168]{1,0:T(8,128)(2,1)} async-done(((bf16[768,1792]{1,0:T(8,128)(2,1)}), bf16[768,7168]{1,0:T(8,128)(2,1)}) %all-gather.2.cloned.1.call-update) | async-done | bytes 11010064 | tf_op jit(solution)/shard_map/all_gather | solution.py:51
  162.5 5.9 %fusion.2 = f32[384,256]{0,1:T(8,128)S(1)} fusion(bf16[768,7168]{1,0:T(8,128)(2,1)} %all-gather.2.cloned.1.call-done, bf16[1,7168,256]{2,1,0:T(8,128)(2,1)} %param.11), kind=kOutput, calls=%fused_computation.6 | convolution fusion | flops 1409286144 | bytes 9568256 | tf_op jit(solution)/shard_map/dot_general | solution.py:55
  168.4 4.9 fusion.4
  173.4 2.1 multiply_reduce_fusion
  175.6 6.5 %psum.7 = f32[8,1,48]{2,1,0:T(1,128)} all-reduce(f32[8,1,48]{2,1,0:T(1,128)S(1)} %all_to_all.23), channel_id=1, replica_groups=mesh['expert'=8,'tensor'=4] {'tensor'}, use_global_device_ids=true, to_apply=%region_8.9 | all-reduce | flops 384 | bytes 3072 | tf_op jit(solution)/shard_map/psum | solution.py:73
  182.1 5.7 %all-to-all-start.4 = ((f32[8,1,48]{2,1,0:T(1,128)}), f32[8,1,48]{2,1,0:T(1,128)S(1)}, u32[]{:S(2)}, u32[]{:S(2)}) async-start(f32[8,1,48]{2,1,0:T(1,128)} %psum.7), calls=%async_computation.5 | async-start | bytes 8192 | tf_op jit(solution)/shard_map/all_to_all | solution.py:82
  187.8 4.0 fusion.6
  191.7 5.7 %convolution_add_fusion = f32[384,7168]{1,0:T(8,128)} fusion(f32[384,7168]{1,0:T(8,128)S(1)} %fusion.6, bf16[1,7168,256]{2,1,0:T(8,128)(2,1)S(1)} %copy-done.3, f32[384,256]{0,1:T(8,128)S(1)} %get-tuple-element.13, f32[384]{0:T(512)S(1)} %reshape.94, f32[384,256]{0,1:T(8,128)S(1)} %fusion.2), kind=kOutput, calls=%fused_computation.2 | convolution fusion | flops 1412726784 | bytes 26478080 | tf_op jit(solution)/shard_map/dot_general | solution.py:70
  197.5 6.0 %all-to-all-start.3 = ((f32[8,48,7168]{2,1,0:T(8,128)}), f32[8,48,7168]{2,1,0:T(8,128)}, u32[]{:S(2)}, u32[]{:S(2)}) async-start(f32[8,48,7168]{2,1,0:T(8,128)} %bitcast.33), calls=%async_computation.3 | async-start | bytes 22020096 | tf_op jit(solution)/shard_map/all_to_all | solution.py:75
  203.8 0.5 broadcast.53
  204.3 0.7 reduce.9
  205.0 1.9 gather_fusion.1
  207.2 0.6 broadcast_select_fusion
  207.9 234.0 %all-to-all-done.3 = f32[8,48,7168]{2,1,0:T(8,128)} async-done(((f32[8,48,7168]{2,1,0:T(8,128)}), f32[8,48,7168]{2,1,0:T(8,128)}, u32[]{:S(2)}, u32[]{:S(2)}) %all-to-all-start.3) | async-done | bytes 11010080 | tf_op jit(solution)/shard_map/all_to_all | solution.py:75
  441.9 13.0 %gather_fusion = f32[256,7168]{1,0:T(8,128)} fusion(f32[384,7168]{1,0:T(8,128)} %bitcast.10, s32[1024]{0:T(1024)S(1)} %pad_clamp_fusion), kind=kCustom, calls=%fused_computation | custom fusion | bytes 14681088 | tf_op jit(solution)/shard_map/jit(_take)/gather | solution.py:91
  454.8 9.3 %reshape.96 = f32[128,2,7168]{2,1,0:T(2,128)} reshape(f32[256,7168]{1,0:T(8,128)} %gather_fusion) | data formatting | bytes 14680064 | tf_op jit(solution)/shard_map/jit(_take)/gather | solution.py:91
  464.1 13.4 %select_reduce_fusion = f32[128,7168]{1,0:T(8,128)} fusion(f32[128,2,7168]{2,1,0:T(2,128)} %reshape.96, pred[128,2]{1,0:T(8,128)(4,1)S(1)} %copy.35), kind=kLoop, calls=%fused_computation.3 | loop fusion | flops 2752512 | bytes 11010304 | tf_op jit(solution)/shard_map/reduce_sum | solution.py:91
  477.6 39.5 %reduce-scatter.2.cloned.1.call-done = f32[128,1792]{1,0:T(8,128)} async-done(((f32[128,7168]{1,0:T(8,128)}), f32[128,1792]{1,0:T(8,128)}) %reduce-scatter.2.cloned.1.call-update) | async-done | bytes 917520 | tf_op jit(solution)/shard_map/reduce_scatter | solution.py:92
  517.1 2.0 convert_element_type.61
  (44 shorter events, 1.6 us)
Async XLA Ops:
  7.2 3.1 copy-start
  11.8 40.1 %all-to-all-start.1 = ((bf16[8,48,1792]{2,1,0:T(8,128)(2,1)}), bf16[8,48,1792]{2,1,0:T(8,128)(2,1)S(1)}, u32[]{:S(2)}, u32[]{:S(2)}) async-start(bf16[8,48,1792]{2,1,0:T(8,128)(2,1)} %bitcast.2), calls=%async_computation.1 | async-start | bytes 2752512 | tf_op jit(solution)/shard_map/all_to_all | solution.py:27
  19.1 143.4 %all-gather.2.cloned.1.call-start = ((), (), s32[]{:S(2)}) async-start(), calls=%async_computation.6 | async-start | bytes 13762560 | tf_op jit(solution)/shard_map/all_gather | solution.py:51
  88.9 1.8 copy-start.5
  162.5 5.9 %copy-start.2 = (bf16[1,7168,256]{2,1,0:T(8,128)(2,1)S(1)}, bf16[1,7168,256]{2,1,0:T(8,128)(2,1)}, u32[]{:S(2)}) copy-start(bf16[1,7168,256]{2,1,0:T(8,128)(2,1)} %param.12) | copy-start | bytes 11010052
  162.5 10.9 %slice-start = ((s8[11010048]{0:T(1024)(128)(4,1)}), s8[4194304]{0:T(1024)(128)(4,1)S(1)}, s32[]{:S(2)}) async-start(s8[11010048]{0:T(1024)(128)(4,1)} %bitcast.37), calls=%async_computation.8 | async-start | bytes 8388608
  162.5 10.9 %slice-start.1 = ((s8[11010048]{0:T(1024)(128)(4,1)}), s8[4194304]{0:T(1024)(128)(4,1)S(1)}, s32[]{:S(2)}) async-start(s8[11010048]{0:T(1024)(128)(4,1)} %bitcast.37), calls=%async_computation.9 | async-start | bytes 8388608
  168.4 5.0 slice-start.2
  168.4 5.0 copy-start.4
  182.1 15.4 %all-to-all-start.4 = ((f32[8,1,48]{2,1,0:T(1,128)}), f32[8,1,48]{2,1,0:T(1,128)S(1)}, u32[]{:S(2)}, u32[]{:S(2)}) async-start(f32[8,1,48]{2,1,0:T(1,128)} %psum.7), calls=%async_computation.5 | async-start | bytes 8192 | tf_op jit(solution)/shard_map/all_to_all | solution.py:82
  187.8 4.0 copy-start.3
  197.5 244.4 %all-to-all-start.3 = ((f32[8,48,7168]{2,1,0:T(8,128)}), f32[8,48,7168]{2,1,0:T(8,128)}, u32[]{:S(2)}, u32[]{:S(2)}) async-start(f32[8,48,7168]{2,1,0:T(8,128)} %bitcast.33), calls=%async_computation.3 | async-start | bytes 22020096 | tf_op jit(solution)/shard_map/all_to_all | solution.py:75
  203.5 313.7 %reduce-scatter.2.cloned.1.call-start = ((), (), s32[]{:S(2)}) async-start(), calls=%async_computation.7 | async-start | bytes 4587520 | tf_op jit(solution)/shard_map/reduce_scatter | solution.py:92
  464.1 55.0 %copy-start.1 = (bf16[128,1792]{1,0:T(8,128)(2,1)S(1)}, bf16[128,1792]{1,0:T(8,128)(2,1)}, u32[]{:S(2)}) copy-start(bf16[128,1792]{1,0:T(8,128)(2,1)} %param.7) | copy-start | bytes 1376260
Sparse Core Ops, SparseCore 0:
  90.8 71.5 all-gather.1
  477.7 39.3 reduce-scatter.1
